TPU v7x, 32 devices: a whole 2x2x4 slice. The times are simulated.
32 devices in a mesh: pipe: 2 (over x), expert: 16 (over z, y, core).
Axes of the slice: x: 2, y: 2, z: 4, core: 2. Of those that a mesh axis runs over, the one named last changes fastest.
Arguments:
- front_tokens: bfloat16 [2, 192, 3584], P('pipe', 'expert'), may hold values from -6 to 6
- front_routes: int32 [2, 192, 2], P('pipe', 'expert'), may hold values from 0 to 1, all different within a row; in each aligned block of 12 rows (0 to 11, 12 to 23, ..., all dimensions but the last counted through in order) at most 12 rows name the same one
- front_mixing: int32 [2, 192, 2], P('pipe', 'expert'), may hold values from 1 to 15
- back_tokens: bfloat16 [2, 192, 3584], P('pipe', 'expert'), may hold values from -6 to 6
- back_routes: int32 [2, 192, 2], P('pipe', 'expert'), may hold values from 0 to 1, all different within a row; in each aligned block of 12 rows (0 to 11, 12 to 23, ..., all dimensions but the last counted through in order) at most 12 rows name the same one
- back_mixing: int32 [2, 192, 2], P('pipe', 'expert'), may hold values from 1 to 15
- back_upstream: bfloat16 [2, 192, 3584], P('pipe', 'expert'), may hold values from -6 to 6
- gate_weight: bfloat16 [2, 3584, 2048], P('pipe', None, 'expert'), may hold values from -0.09375 to 0.09375
- up_weight: bfloat16 [2, 3584, 2048], P('pipe', None, 'expert'), may hold values from -0.09375 to 0.09375
- down_weight: bfloat16 [2, 2048, 3584], P('pipe', 'expert'), may hold values from -0.1875 to 0.1875
Outputs:
- front_result: bfloat16 [2, 192, 3584], P('pipe', 'expert')
- token_grads: bfloat16 [2, 192, 3584], P('pipe', 'expert')
- gate_grads: bfloat16 [2, 1792, 2048], P('pipe', None, 'expert')
- up_grads: bfloat16 [2, 1792, 2048], P('pipe', None, 'expert')
- down_grads: bfloat16 [2, 2048, 1792], P('pipe', 'expert')
Inputs may be any that keep to these rules, and one draw needn't show every extreme that they name: `front_routes`: each row names 2 different experts; within each device's block of 12 rows no expert is named more than 12 times, a bound that some block reaches. `back_routes`: each row names 2 different experts; within each device's block of 12 rows no expert is named more than 12 times, a bound that some block reaches.
All inputs are finite; a program needn't handle non-finite values.
Results may differ from a plain program's by a relative error of at most 0.0071.
Values may be sent and summed in bfloat16 or wider, within the bound.
A program may use at most 64 MiB of HBM per device.

v0:
```python
import jax
import jax.numpy as jnp
from jax import lax
from jax.sharding import PartitionSpec as P

SHARDS = 8


weight_unit = 0.0625


def hit_tables(routes, mixing, experts, capacity):
    token_count, route_count = routes.shape
    flat_routes = routes.reshape(token_count * route_count)
    matches = (flat_routes[:, None] == jnp.arange(experts, dtype=jnp.int32)[None, :]).astype(
        jnp.int32
    )
    earlier = jnp.cumsum(matches, axis=0) - matches
    position = jnp.sum(earlier * matches, axis=1)
    slot_ids = flat_routes * capacity + position
    hit_table = (
        slot_ids[:, None] == jnp.arange(experts * capacity, dtype=jnp.int32)[None, :]
    ).astype(jnp.float32)
    hit_table = hit_table.reshape(token_count, route_count, experts * capacity)
    weights = mixing.astype(jnp.float32) * weight_unit
    picker = jnp.sum(hit_table, axis=1)
    mix_table = jnp.sum(hit_table * weights[:, :, None], axis=1)
    return (picker, mix_table)


def deliver(slot_rows, experts, capacity):
    stacks = slot_rows.shape[0]
    feature_count = slot_rows.shape[2]
    copies = jnp.repeat(slot_rows.reshape(stacks, experts, capacity, feature_count), SHARDS, axis=1)
    landed = lax.all_to_all(copies, "expert", split_axis=1, concat_axis=1, tiled=True)
    return landed.reshape(stacks, experts * SHARDS * capacity, feature_count)


def collect(shard_parts, experts, capacity):
    feature_count = shard_parts.shape[1]
    sources = experts * SHARDS
    returned = lax.all_to_all(
        shard_parts.reshape(sources, capacity, feature_count),
        "expert",
        split_axis=0,
        concat_axis=0,
        tiled=True,
    )
    summed = jnp.sum(
        returned.reshape(experts, SHARDS, capacity, feature_count).astype(jnp.float32), axis=1
    )
    result_rows = summed.astype(jnp.bfloat16).reshape(experts * capacity, feature_count)
    return result_rows


def mirror_move(values, split_dim, concat_dim):
    return lax.all_to_all(values, "pipe", split_axis=split_dim, concat_axis=concat_dim, tiled=True)


def local(
    front_tokens,
    front_routes,
    front_mixing,
    back_tokens,
    back_routes,
    back_mixing,
    back_upstream,
    gate_weight,
    up_weight,
    down_weight,
):
    experts = lax.axis_size("expert") // SHARDS
    token_count = front_tokens.shape[1]
    route_count = front_routes.shape[2]
    feature_count = front_tokens.shape[2]
    capacity = min(token_count, max(2, 3 * token_count * route_count // (2 * experts)))
    front_pick, front_mix = hit_tables(front_routes[0], front_mixing[0], experts, capacity)
    back_pick, back_mix = hit_tables(back_routes[0], back_mixing[0], experts, capacity)
    front_slots = jnp.dot(
        front_pick.T.astype(jnp.bfloat16), front_tokens[0], preferred_element_type=jnp.float32
    ).astype(jnp.bfloat16)
    back_slots = jnp.dot(
        back_pick.T.astype(jnp.bfloat16), back_tokens[0], preferred_element_type=jnp.float32
    ).astype(jnp.bfloat16)
    scaled_slots = jnp.dot(
        back_mix.T, back_upstream[0].astype(jnp.float32), precision=lax.Precision.HIGHEST
    ).astype(jnp.bfloat16)
    landed = deliver(jnp.stack([front_slots, back_slots, scaled_slots]), experts, capacity)
    gate_cols = gate_weight[0]
    up_cols = up_weight[0]
    down_rows = down_weight[0]
    front_rows = landed[0]
    front_gate = jnp.dot(front_rows, gate_cols, preferred_element_type=jnp.float32)
    front_up = jnp.dot(front_rows, up_cols, preferred_element_type=jnp.float32)
    front_hidden = (jax.nn.silu(front_gate) * front_up).astype(jnp.bfloat16)
    front_parts = jnp.dot(front_hidden, down_rows, preferred_element_type=jnp.float32).astype(
        jnp.bfloat16
    )
    front_summed = collect(front_parts, experts, capacity)
    front_result = jnp.dot(
        front_mix, front_summed.astype(jnp.float32), precision=lax.Precision.HIGHEST
    ).astype(jnp.bfloat16)
    back_rows = landed[1]
    scaled_rows = landed[2]
    back_gate = jnp.dot(back_rows, gate_cols, preferred_element_type=jnp.float32)
    back_up = jnp.dot(back_rows, up_cols, preferred_element_type=jnp.float32)
    gate_act = jax.nn.silu(back_gate)
    gate_sig = jax.nn.sigmoid(back_gate)
    back_hidden = (gate_act * back_up).astype(jnp.bfloat16)
    down_section = jnp.dot(scaled_rows.T, back_hidden, preferred_element_type=jnp.float32).astype(
        jnp.bfloat16
    )
    hidden_grad = jnp.dot(scaled_rows, down_rows.T, preferred_element_type=jnp.float32)
    act_slope = gate_sig * (1.0 + back_gate * (1.0 - gate_sig))
    gate_delta = (hidden_grad * back_up * act_slope).astype(jnp.bfloat16)
    up_delta = (hidden_grad * gate_act).astype(jnp.bfloat16)
    gate_section = jnp.dot(back_rows.T, gate_delta, preferred_element_type=jnp.float32).astype(
        jnp.bfloat16
    )
    up_section = jnp.dot(back_rows.T, up_delta, preferred_element_type=jnp.float32).astype(
        jnp.bfloat16
    )
    back_parts = (
        jnp.dot(gate_delta, gate_cols.T, preferred_element_type=jnp.float32)
        + jnp.dot(up_delta, up_cols.T, preferred_element_type=jnp.float32)
    ).astype(jnp.bfloat16)
    grad_slots = collect(back_parts, experts, capacity)
    token_grads = jnp.dot(
        back_pick.astype(jnp.bfloat16), grad_slots, preferred_element_type=jnp.float32
    ).astype(jnp.bfloat16)
    section_grads = lax.optimization_barrier(jnp.stack([gate_section, up_section, down_section]))
    pipe_count = lax.axis_size("pipe")
    half_rows = feature_count // 2
    upper_half = lax.axis_index("pipe") * 2 >= pipe_count
    own_half = jnp.where(upper_half, section_grads[:, half_rows:], section_grads[:, :half_rows])
    leaving = jnp.where(upper_half, section_grads[:, :half_rows], section_grads[:, half_rows:])
    piece_rows = half_rows // pipe_count
    spread_out = mirror_move(leaving, 1, 0)
    by_source = spread_out.reshape(pipe_count, 3, piece_rows, leaving.shape[2])
    reversed_sources = jnp.flip(by_source, axis=0).reshape(
        pipe_count * 3, piece_rows, leaving.shape[2]
    )
    leaving = mirror_move(reversed_sources, 0, 1)
    summed = (own_half.astype(jnp.float32) + leaving.astype(jnp.float32)).astype(jnp.bfloat16)
    return (
        front_result[None],
        token_grads[None],
        summed[0][None],
        summed[1][None],
        summed[2].T[None],
    )


def solution(mesh):
    placed = (
        P("pipe", "expert", None),
        P("pipe", "expert", None),
        P("pipe", "expert", None),
        P("pipe", "expert", None),
        P("pipe", "expert", None),
        P("pipe", "expert", None),
        P("pipe", "expert", None),
        P("pipe", None, "expert"),
        P("pipe", None, "expert"),
        P("pipe", "expert", None),
    )
    return jax.shard_map(
        local,
        mesh=mesh,
        in_specs=placed,
        out_specs=(
            P("pipe", "expert", None),
            P("pipe", "expert", None),
            P("pipe", None, "expert"),
            P("pipe", None, "expert"),
            P("pipe", "expert", None),
        ),
        check_vma=False,
    )
```

profile of v0, /device:TPU:0, one launch (start us, length us, event | category | flops | bytes accessed | tf_op | source)
XLA Modules:
  0.0 308.7 jit_solution(14618682792077326766)
XLA Ops:
  0.7 0.9 copy.61
  6.7 1.2 convolution_convert_fusion.4
  8.0 1.1 convolution_convert_fusion.5
  9.8 3.1 %broadcast_in_dim.8 = bf16[3,2,8,12,3584]{4,3,0,2,1:T(8,128)(2,1)} broadcast(bf16[3,2,12,3584]{3,2,0,1:T(8,128)(2,1)S(1)} %copy.69), dimensions={0,1,3,4} | broadcast | bytes 4644864 | tf_op jit(solution)/shard_map/broadcast_in_dim | solution.py:34
  12.9 7.4 %all-to-all-start = ((bf16[3,16,12,3584]{3,2,0,1:T(8,128)(2,1)}), bf16[3,16,12,3584]{3,2,0,1:T(8,128)(2,1)}, u32[]{:S(2)}, u32[]{:S(2)}) async-start(bf16[3,16,12,3584]{3,2,0,1:T(8,128)(2,1)} %bitcast.97), calls=%async_computation | async-start | bytes 11010048 | tf_op jit(solution)/shard_map/all_to_all | solution.py:35
  20.3 100.5 %all-to-all-done = bf16[3,16,12,3584]{3,2,0,1:T(8,128)(2,1)} async-done(((bf16[3,16,12,3584]{3,2,0,1:T(8,128)(2,1)}), bf16[3,16,12,3584]{3,2,0,1:T(8,128)(2,1)}, u32[]{:S(2)}, u32[]{:S(2)}) %all-to-all-start) | async-done | bytes 4128800 | tf_op jit(solution)/shard_map/all_to_all | solution.py:35
  120.8 5.2 %fusion.40 = (bf16[1,16,12,3584]{3,2,0,1:T(8,128)(2,1)}, bf16[1,16,12,3584]{3,2,0,1:T(8,128)(2,1)}, bf16[1,16,12,3584]{3,2,0,1:T(8,128)(2,1)}) fusion(bf16[3,16,12,3584]{3,2,0,1:T(8,128)(2,1)} %all-to-all-done), kind=kLoop, calls=%fused_computation.75 | loop fusion | bytes 8257536 | tf_op jit(solution)/shard_map/slice | solution.py:104
  126.0 2.4 squeeze.40
  129.5 3.4 %squeeze.39 = bf16[192,3584]{1,0:T(8,128)(2,1)} reshape(bf16[1,16,12,3584]{3,2,0,1:T(8,128)(2,1)} %get-tuple-element.34) | data formatting | bytes 2752512 | tf_op jit(solution)/shard_map/squeeze | solution.py:104
  132.9 2.2 fusion.3
  137.6 1.4 copy-done.1
  139.0 8.5 %copy.70 = bf16[3,1792,128]{2,0,1:T(4,128)(2,1)S(1)} copy(bf16[3,1792,128]{2,1,0:T(8,128)(2,1)S(1)} %broadcast_select_fusion) | data formatting | bytes 2752512 | tf_op jit(solution)/shard_map/jit(_where)/select_n | solution.py:136
  147.5 25.8 %all_to_all.39 = bf16[3,1792,128]{2,0,1:T(4,128)(2,1)S(1)} all-to-all(bf16[3,1792,128]{2,0,1:T(4,128)(2,1)S(1)} %copy.70), channel_id=1, replica_groups=mesh['pipe'=2,'expert'=16] {'pipe'}, dimensions={1} | all-to-all | bytes 2752512 | tf_op jit(solution)/shard_map/all_to_all | solution.py:57
  173.4 1.2 reverse.3
  174.6 2.5 copy.72
  177.1 4.8 %all-to-all-start.4 = ((bf16[6,896,128]{2,1,0:T(8,128)(2,1)}), bf16[6,896,128]{2,1,0:T(8,128)(2,1)}, u32[]{:S(2)}, u32[]{:S(2)}) async-start(bf16[6,896,128]{2,1,0:T(8,128)(2,1)} %bitcast.20), calls=%async_computation.4 | async-start | bytes 2752512 | tf_op jit(solution)/shard_map/all_to_all | solution.py:57
  181.9 2.4 squeeze.35
  184.8 3.2 %convolution_convert_fusion = bf16[192,3584]{1,0:T(8,128)(2,1)} fusion(bf16[192,3584]{1,0:T(8,128)(2,1)S(1)} %squeeze.35, bf16[1,128,3584]{2,1,0:T(8,128)(2,1)} %param.19, bf16[1,3584,128]{2,1,0:T(8,128)(2,1)S(1)} %copy-done, f32[192,128]{1,0:T(8,128)S(1)} %fusion.20), kind=kOutput, calls=%fused_computation.2 | convolution fusion | flops 353157120 | bytes 4685824 | tf_op jit(solution)/shard_map/dot_general | solution.py:96
  188.0 3.3 %reshape.117 = bf16[16,12,3584]{2,1,0:T(8,128)(2,1)} reshape(bf16[192,3584]{1,0:T(8,128)(2,1)} %convolution_convert_fusion) | data formatting | bytes 2752512 | tf_op jit(solution)/shard_map/reshape | solution.py:43
  191.3 7.9 %all-to-all-done.4 = bf16[6,896,128]{2,1,0:T(8,128)(2,1)} async-done(((bf16[6,896,128]{2,1,0:T(8,128)(2,1)}), bf16[6,896,128]{2,1,0:T(8,128)(2,1)}, u32[]{:S(2)}, u32[]{:S(2)}) %all-to-all-start.4) | async-done | bytes 1376288 | tf_op jit(solution)/shard_map/all_to_all | solution.py:57
  199.2 24.1 %all-to-all-start.1 = ((bf16[16,12,3584]{2,1,0:T(8,128)(2,1)}), bf16[16,12,3584]{2,1,0:T(8,128)(2,1)}, u32[]{:S(2)}, u32[]{:S(2)}) async-start(bf16[16,12,3584]{2,1,0:T(8,128)(2,1)} %reshape.117), calls=%async_computation.1 | async-start | bytes 3670016 | tf_op jit(solution)/shard_map/all_to_all | solution.py:42
  224.4 1.4 reshape.120
  225.8 34.1 %all-to-all-done.1 = bf16[16,12,3584]{2,1,0:T(8,128)(2,1)} async-done(((bf16[16,12,3584]{2,1,0:T(8,128)(2,1)}), bf16[16,12,3584]{2,1,0:T(8,128)(2,1)}, u32[]{:S(2)}, u32[]{:S(2)}) %all-to-all-start.1) | async-done | bytes 1376288 | tf_op jit(solution)/shard_map/all_to_all | solution.py:42
  259.9 10.2 %all-to-all-start.2 = ((bf16[16,12,3584]{2,1,0:T(8,128)(2,1)}), bf16[16,12,3584]{2,1,0:T(8,128)(2,1)S(1)}, u32[]{:S(2)}, u32[]{:S(2)}) async-start(bf16[16,12,3584]{2,1,0:T(8,128)(2,1)} %reshape.120), calls=%async_computation.2 | async-start | bytes 3670016 | tf_op jit(solution)/shard_map/all_to_all | solution.py:42
  270.1 1.5 convert_bitcast_fusion
  271.8 1.6 copy-done.2
  273.8 1.0 slice_bitcast_fusion
  274.8 1.0 copy.74
  275.8 1.8 bitcast_reduce_fusion.1
  277.7 28.9 %all-to-all-done.2 = bf16[16,12,3584]{2,1,0:T(8,128)(2,1)S(1)} async-done(((bf16[16,12,3584]{2,1,0:T(8,128)(2,1)}), bf16[16,12,3584]{2,1,0:T(8,128)(2,1)S(1)}, u32[]{:S(2)}, u32[]{:S(2)}) %all-to-all-start.2) | async-done | bytes 1376288 | tf_op jit(solution)/shard_map/all_to_all | solution.py:42
  307.0 0.8 fusion.5
  307.8 0.9 fusion.4
  (57 shorter events, 12.0 us)
Async XLA Ops:
  0.6 128.3 %copy-start = (bf16[1,3584,128]{2,1,0:T(8,128)(2,1)S(1)}, bf16[1,3584,128]{2,1,0:T(8,128)(2,1)}, u32[]{:S(2)}) copy-start(bf16[1,3584,128]{2,1,0:T(8,128)(2,1)} %param.18) | copy-start | bytes 2752516
  0.6 8.7 %copy-start.6 = (bf16[1,12,3584]{2,1,0:T(8,128)(2,1)S(1)}, bf16[1,12,3584]{2,1,0:T(8,128)(2,1)}, u32[]{:S(2)}) copy-start(bf16[1,12,3584]{2,1,0:T(8,128)(2,1)} %param.10) | copy-start | bytes 258052
  12.9 107.9 %all-to-all-start = ((bf16[3,16,12,3584]{3,2,0,1:T(8,128)(2,1)}), bf16[3,16,12,3584]{3,2,0,1:T(8,128)(2,1)}, u32[]{:S(2)}, u32[]{:S(2)}) async-start(bf16[3,16,12,3584]{3,2,0,1:T(8,128)(2,1)} %bitcast.97), calls=%async_computation | async-start | bytes 11010048 | tf_op jit(solution)/shard_map/all_to_all | solution.py:35
  126.0 2.5 copy-start.3
  132.9 2.2 copy-start.4
  132.9 2.2 copy-start.5
  137.4 1.6 copy-start.1
  177.1 22.1 %all-to-all-start.4 = ((bf16[6,896,128]{2,1,0:T(8,128)(2,1)}), bf16[6,896,128]{2,1,0:T(8,128)(2,1)}, u32[]{:S(2)}, u32[]{:S(2)}) async-start(bf16[6,896,128]{2,1,0:T(8,128)(2,1)} %bitcast.20), calls=%async_computation.4 | async-start | bytes 2752512 | tf_op jit(solution)/shard_map/all_to_all | solution.py:57
  199.2 60.7 %all-to-all-start.1 = ((bf16[16,12,3584]{2,1,0:T(8,128)(2,1)}), bf16[16,12,3584]{2,1,0:T(8,128)(2,1)}, u32[]{:S(2)}, u32[]{:S(2)}) async-start(bf16[16,12,3584]{2,1,0:T(8,128)(2,1)} %reshape.117), calls=%async_computation.1 | async-start | bytes 3670016 | tf_op jit(solution)/shard_map/all_to_all | solution.py:42
  259.9 46.7 %all-to-all-start.2 = ((bf16[16,12,3584]{2,1,0:T(8,128)(2,1)}), bf16[16,12,3584]{2,1,0:T(8,128)(2,1)S(1)}, u32[]{:S(2)}, u32[]{:S(2)}) async-start(bf16[16,12,3584]{2,1,0:T(8,128)(2,1)} %reshape.120), calls=%async_computation.2 | async-start | bytes 3670016 | tf_op jit(solution)/shard_map/all_to_all | solution.py:42
  271.6 1.8 copy-start.2
where the time goes:
time: 314 us; the launch traced here: 309 us
  waiting for transfers between devices  171 us (54%)
  starting transfers between devices  46.4 us (15%)
  local copies, waits for them, and re-layouts  41.6 us (13%)
  blocking collectives  25.8 us (8%)
  matrix products  14.2 us (5%)
  other arithmetic  8.21 us (3%)
    all_to_all x1, waiting for transfers between devices, deliver(): lax.all_to_all(copies, 'expert', split_axis=1, concat_axis=1, tiled=True)  100 us
    all_to_all x2, waiting for transfers between devices, collect(): lax.all_to_all(shard_parts.reshape(sources, capacity, feature_count), 'ex...  63 us
    all_to_all x2, starting transfers between devices, collect(): lax.all_to_all(shard_parts.reshape(sources, capacity, feature_count), 'ex...  34.2 us
    all_to_all x1, blocking collectives, mirror_move(): lax.all_to_all(values, 'pipe', split_axis=split_dim, concat_axis=concat_d...  25.8 us
    select_n x1, local copies, waits for them, and re-layouts, local(): jnp.where(upper_half, section_grads[:, :half_rows], section_grads[:, half...  8.52 us
    all_to_all x1, waiting for transfers between devices, mirror_move(): lax.all_to_all(values, 'pipe', split_axis=split_dim, concat_axis=concat_d...  7.95 us
    all_to_all x1, starting transfers between devices, deliver(): lax.all_to_all(copies, 'expert', split_axis=1, concat_axis=1, tiled=True)  7.43 us
  transfers between devices with their start and end apart: 4, of which 4 were waited for; matrix products, arithmetic and copies ran while one was open for 6% of the time, Pallas kernels for 0%

commit v1 on v0

v1 whole, which is shorter than its diff:
```python
import jax
import jax.numpy as jnp
from jax import lax
from jax.sharding import PartitionSpec as P

SHARDS = 8
LANES = 128

weight_unit = 0.0625


def token_weights(routes, mixing):
    hits = routes[:, :, None] == jnp.arange(LANES, dtype=jnp.int32)[None, None, :]
    weights = mixing.astype(jnp.float32) * weight_unit
    return jnp.sum(jnp.where(hits, weights[:, :, None], 0.0), axis=1).astype(jnp.bfloat16)


def rows_dot(rows, matrix, dim):
    return lax.dot_general(
        rows, matrix, (((2,), (dim,)), ((), ())), preferred_element_type=jnp.float32
    )


def grad_dot(rows, deltas):
    return lax.dot_general(
        rows, deltas, (((0, 1), (0, 1)), ((), ())), preferred_element_type=jnp.float32
    ).astype(jnp.bfloat16)


def local(
    front_tokens,
    front_routes,
    front_mixing,
    back_tokens,
    back_routes,
    back_mixing,
    back_upstream,
    gate_weight,
    up_weight,
    down_weight,
):
    tokens = front_tokens.shape[1]
    features = front_tokens.shape[2]
    gate_cols = gate_weight[0]
    up_cols = up_weight[0]
    down_rows = down_weight[0]
    expert = lax.axis_index("expert") // SHARDS
    picked = (jnp.arange(LANES, dtype=jnp.int32) == expert).astype(jnp.float32)

    front_table = token_weights(front_routes[0], front_mixing[0])
    back_table = token_weights(back_routes[0], back_mixing[0])
    back_load = jnp.concatenate(
        [
            jnp.concatenate([back_tokens[0], jnp.zeros_like(back_table)], axis=1),
            jnp.concatenate([back_upstream[0], back_table], axis=1),
        ],
        axis=0,
    )
    front_load = jnp.concatenate([front_tokens[0], front_table], axis=1)
    back_all = lax.all_gather(back_load, "expert", axis=0)
    front_all = lax.all_gather(front_load, "expert", axis=0)

    def own_weight(table):
        return jnp.sum(table.astype(jnp.float32) * picked, axis=2, keepdims=True)

    back_rows = back_all[:, :tokens, :features]
    upstream = back_all[:, tokens:, :features]
    back_scale = own_weight(back_all[:, tokens:, features:])
    scaled_rows = (upstream.astype(jnp.float32) * back_scale).astype(jnp.bfloat16)
    back_gate = rows_dot(back_rows, gate_cols, 0)
    back_up = rows_dot(back_rows, up_cols, 0)
    hidden_grad = rows_dot(scaled_rows, down_rows, 1)
    gate_sig = jax.nn.sigmoid(back_gate)
    gate_act = back_gate * gate_sig
    back_hidden = (gate_act * back_up).astype(jnp.bfloat16)
    act_slope = gate_sig * (1.0 + back_gate * (1.0 - gate_sig))
    gate_delta = (hidden_grad * back_up * act_slope).astype(jnp.bfloat16)
    up_delta = (hidden_grad * gate_act).astype(jnp.bfloat16)
    sections = jnp.stack(
        [
            grad_dot(back_rows, gate_delta),
            grad_dot(back_rows, up_delta),
            grad_dot(scaled_rows, back_hidden),
        ]
    )
    pipe_count = lax.axis_size("pipe")
    half = features // 2
    upper = lax.axis_index("pipe") * 2 >= pipe_count
    own_start = jnp.where(upper, half, 0)
    own_half = lax.dynamic_slice_in_dim(sections, own_start, half, axis=1)
    leaving = lax.dynamic_slice_in_dim(sections, half - own_start, half, axis=1)
    arrived = lax.ppermute(leaving, "pipe", [(p, pipe_count - 1 - p) for p in range(pipe_count)])

    back_parts = (rows_dot(gate_delta, gate_cols, 1) + rows_dot(up_delta, up_cols, 1)).astype(
        jnp.bfloat16
    )
    front_rows = front_all[:, :, :features]
    front_scale = own_weight(front_all[:, :, features:])
    front_gate = rows_dot(front_rows, gate_cols, 0)
    front_up = rows_dot(front_rows, up_cols, 0)
    front_hidden = (jax.nn.silu(front_gate) * front_up).astype(jnp.bfloat16)
    front_parts = (rows_dot(front_hidden, down_rows, 0) * front_scale).astype(jnp.bfloat16)
    totals = lax.psum_scatter(
        jnp.concatenate([front_parts, back_parts], axis=1), "expert", scatter_dimension=0
    )
    summed = (own_half.astype(jnp.float32) + arrived.astype(jnp.float32)).astype(jnp.bfloat16)
    return (
        totals[:tokens][None],
        totals[tokens:][None],
        summed[0][None],
        summed[1][None],
        summed[2].T[None],
    )


def solution(mesh):
    rows = P("pipe", "expert", None)
    columns = P("pipe", None, "expert")
    return jax.shard_map(
        local,
        mesh=mesh,
        in_specs=(rows,) * 7 + (columns, columns, rows),
        out_specs=(rows, rows, columns, columns, rows),
        check_vma=False,
    )
```

time: 314 us -> 192 us (0.61); the launches traced: 309 us -> 192 us
  starting transfers between devices: 46.4 us -> 1.63 us
  waiting for transfers between devices: 171 us -> 137 us
  blocking collectives: 25.8 us -> 0 us
  local copies, waits for them, and re-layouts: 41.6 us -> 16.5 us
  between operations: 0.97 us -> 13.9 us
    all_to_all x4 -> x0, waiting for transfers between devices: 171 us -> none  [the longest x1 100 us: deliver(): lax.all_to_all(copies, 'expert', split_axis=1, concat_axis=1, tiled=True)]
    all_gather x0 -> x2, waiting for transfers between devices: none -> 83.3 us  [the longest x1 43 us: local(): back_all = lax.all_gather(back_load, 'expert', axis=0)]
    all_to_all x4 -> x0, starting transfers between devices: 46.4 us -> none  [the longest x2 34.2 us: collect(): lax.all_to_all(shard_parts.reshape(sources, capacity, feature_count), 'ex...]
    ppermute x0 -> x1, waiting for transfers between devices: none -> 30.9 us  [local(): lax.ppermute(leaving, 'pipe', [(p, pipe_count - 1 - p) for p in range(pip...]
    all_to_all x1 -> x0, blocking collectives: 25.8 us -> none  [mirror_move(): lax.all_to_all(values, 'pipe', split_axis=split_dim, concat_axis=concat_d...]
    reduce_scatter x0 -> x1, waiting for transfers between devices: none -> 22.3 us  [local(): lax.psum_scatter(jnp.concatenate([front_parts, back_parts], axis=1), 'exp...]
    select_n x1 -> x0, local copies, waits for them, and re-layouts: 8.52 us -> none  [local(): jnp.where(upper_half, section_grads[:, :half_rows], section_grads[:, half...]
    squeeze x3 -> x0, local copies, waits for them, and re-layouts: 8.25 us -> none  [the longest x1 3.43 us: local(): scaled_rows = landed[2]]
where the time goes in v1:
time: 192 us
  waiting for transfers between devices  137 us (71%)
  matrix products  17.2 us (9%)
  local copies, waits for them, and re-layouts  16.5 us (9%)
  between operations  13.9 us (7%)
  other arithmetic  5.92 us (3%)
    all_gather x1, waiting for transfers between devices, local(): back_all = lax.all_gather(back_load, 'expert', axis=0)  43 us
    all_gather x1, waiting for transfers between devices, local(): front_all = lax.all_gather(front_load, 'expert', axis=0)  40.3 us
    ppermute x1, waiting for transfers between devices, local(): lax.ppermute(leaving, 'pipe', [(p, pipe_count - 1 - p) for p in range(pip...  30.9 us
    reduce_scatter x1, waiting for transfers between devices, local(): lax.psum_scatter(jnp.concatenate([front_parts, back_parts], axis=1), 'exp...  22.3 us
    dot_general x7, matrix products, rows_dot(): lax.dot_general(rows, matrix, (((2,), (dim,)), ((), ())), preferred_eleme...  13.8 us
  transfers between devices with their start and end apart: 4, of which 4 were waited for; matrix products, arithmetic and copies ran while one was open for 6% of the time, Pallas kernels for 0%

profile of v1, /device:TPU:0, one launch (start us, length us, event | category | flops | bytes accessed | tf_op | source)
XLA Modules:
  0.0 191.8 jit_solution(6326186555777506738)
XLA Ops:
  7.2 0.8 multiply_bitcast_fusion.1
  8.1 0.8 copy.75
  9.0 1.6 maximum_bitcast_fusion
  10.6 0.7 multiply_bitcast_fusion
  11.4 0.8 copy.81
  12.2 1.7 fusion.31
  14.0 40.3 %all-gather.8.cloned.1.call-done = bf16[16,12,3712]{2,1,0:T(8,128)(2,1)} async-done(((bf16[1,12,3712]{2,1,0:T(8,128)(2,1)}), bf16[16,12,3712]{2,1,0:T(8,128)(2,1)}) %all-gather.8.cloned.1.call-update) | async-done | bytes 1425424 | tf_op jit(solution)/shard_map/all_gather | solution.py:61
  54.4 1.7 slice.42
  56.1 1.0 fusion.12
  57.1 43.0 %all-gather.6.cloned.1.call-done = bf16[384,3712]{1,0:T(8,128)(2,1)} async-done(((bf16[24,3712]{1,0:T(8,128)(2,1)}), bf16[384,3712]{1,0:T(8,128)(2,1)}) %all-gather.6.cloned.1.call-update) | async-done | bytes 2850832 | tf_op jit(solution)/shard_map/all_gather | solution.py:60
  100.0 0.9 slice.45
  100.9 2.9 %slice.46 = bf16[16,12,3584]{2,1,0:T(8,128)(2,1)} slice(bf16[16,24,3712]{2,1,0:T(8,128)(2,1)} %bitcast.72), slice={[0:16], [0:12], [0:3584]} | slice | bytes 2752512 | tf_op jit(solution)/shard_map/slice | solution.py:66
  104.0 2.6 %fusion.8 = f32[16,12,128]{2,1,0:T(8,128)S(1)} fusion(bf16[16,24,3712]{2,1,0:T(8,128)(2,1)} %bitcast.73, f32[16,12]{1,0:T(8,128)S(1)} %copy.84, bf16[1,128,3584]{2,1,0:T(8,128)(2,1)} %param.19), kind=kOutput, calls=%fused_computation.17 | convolution fusion | flops 178225152 | bytes 2851584 | tf_op jit(solution)/shard_map/dot_general | solution.py:19
  106.7 1.0 fusion.17
  107.8 1.0 multiply_convert_fusion.4
  108.8 2.1 %fusion.21 = f32[16,12,3584]{2,0,1:T(8,128)} fusion(bf16[16,12,128]{2,0,1:T(8,128)(2,1)S(1)} %get-tuple-element.41, bf16[1,3584,128]{2,1,0:T(8,128)(2,1)S(1)} %copy-done.6), kind=kOutput, calls=%fused_computation.29 | convolution fusion | flops 176160768 | bytes 3719168 | tf_op jit(solution)/shard_map/dot_general | solution.py:19
  110.9 3.8 %fusion = bf16[16,12,3584]{2,0,1:T(8,128)(2,1)} fusion(f32[16,12]{0,1:T(8,128)S(1)} %get-tuple-element.35, bf16[16,12,3584]{2,1,0:T(8,128)(2,1)S(1)} %slice.42, bf16[1,128,3584]{2,1,0:T(8,128)(2,1)} %param.19, bf16[1,3584,128]{2,1,0:T(8,128)(2,1)S(1)} %copy-done, f32[16,12,128]{2,0,1:T(8,128)S(1)} %fusion.12), kind=kOutput, calls=%fused_computation.2 | convolution fusion | flops 353845248 | bytes 4686592 | tf_op jit(solution)/shard_map/dot_general | solution.py:19
  114.7 2.4 %fusion.1 = bf16[16,12,3584]{2,0,1:T(8,128)(2,1)S(1)} fusion(f32[16,12,3584]{2,0,1:T(8,128)} %fusion.21, bf16[16,12,128]{2,0,1:T(8,128)(2,1)S(1)} %get-tuple-element.40, bf16[1,3584,128]{2,1,0:T(8,128)(2,1)S(1)} %copy-done), kind=kOutput, calls=%fused_computation.3 | convolution fusion | flops 177537024 | bytes 5095424 | tf_op jit(solution)/shard_map/dot_general | solution.py:19
  117.4 3.1 %copy.88 = bf16[16,24,3584]{2,1,0:T(8,128)(2,1)} copy(bf16[16,24,3584]{2,0,1:T(8,128)(2,1)S(1)} %pad_maximum_fusion) | data formatting | bytes 5505024 | tf_op jit(solution)/shard_map/concatenate | solution.py:104
  120.5 1.5 copy-done.3
  121.9 1.2 fusion.6
  123.2 1.2 fusion.7
  124.4 0.7 copy-done.4
  125.1 0.9 fusion.5
  126.0 0.3 pad_maximum_fusion.1
  126.5 1.5 collective-permute-start
  128.0 30.9 %collective-permute-done = bf16[3,1792,128]{2,1,0:T(8,128)(2,1)S(1)} collective-permute-done((bf16[3,1792,128]{2,1,0:T(8,128)(2,1)S(1)}, bf16[3,1792,128]{2,1,0:T(8,128)(2,1)S(1)}, u32[]{:S(2)}, u32[]{:S(2)}) %collective-permute-start) | collective-permute-done | bytes 1376288 | tf_op jit(solution)/shard_map/ppermute | solution.py:92
  158.9 0.4 add_convert_fusion
  159.2 1.0 slice_bitcast_fusion
  160.2 1.0 copy.90
  161.2 22.3 %reduce-scatter.2.cloned.1.call-done = bf16[1,24,3584]{2,1,0:T(8,128)(2,1)} async-done(((bf16[16,24,3584]{2,1,0:T(8,128)(2,1)}), bf16[1,24,3584]{2,1,0:T(8,128)(2,1)}) %reduce-scatter.2.cloned.1.call-update) | async-done | bytes 172048 | tf_op jit(solution)/shard_map/reduce_scatter | solution.py:103
  183.5 1.7 fusion.43
  (29 shorter events, 1.4 us)
Async XLA Ops:
  7.2 99.5 %copy-start = (bf16[1,3584,128]{2,1,0:T(8,128)(2,1)S(1)}, bf16[1,3584,128]{2,1,0:T(8,128)(2,1)}, u32[]{:S(2)}) copy-start(bf16[1,3584,128]{2,1,0:T(8,128)(2,1)} %param.18) | copy-start | bytes 2752516
  7.2 47.2 %all-gather.8.cloned.1.call-start = ((), (), s32[]{:S(2)}) async-start(), calls=%async_computation.3 | async-start | bytes 2019328 | tf_op jit(solution)/shard_map/all_gather | solution.py:61
  10.5 89.5 %all-gather.6.cloned.1.call-start = ((), (), s32[]{:S(2)}) async-start(), calls=%async_computation.2 | async-start | bytes 3028992 | tf_op jit(solution)/shard_map/all_gather | solution.py:60
  14.0 169.6 %reduce-scatter.2.cloned.1.call-start = ((), (), s32[]{:S(2)}) async-start(), calls=%async_computation.1 | async-start | bytes 2924544 | tf_op jit(solution)/shard_map/reduce_scatter | solution.py:103
  54.4 1.7 copy-start.5
  100.9 2.9 %slice-start = ((bf16[16,12,3712]{2,1,0:T(8,128)(2,1)}), bf16[16,12,128]{2,1,0:T(8,128)(2,1)S(1)}, s32[]{:S(2)}) async-start(bf16[16,12,3712]{2,1,0:T(8,128)(2,1)} %all-gather.8.cloned.1.call-done), calls=%async_computation.4 | async-start | bytes 131072 | tf_op jit(solution)/shard_map/slice | solution.py:98
  104.0 2.6 %copy-start.2 = (bf16[16,12,3584]{2,1,0:T(8,128)(2,1)S(1)}, bf16[16,12,3584]{2,1,0:T(8,128)(2,1)}, u32[]{:S(2)}) copy-start(bf16[16,12,3584]{2,1,0:T(8,128)(2,1)} %slice.46) | copy-start | bytes 4128772
  106.7 1.2 copy-start.6
  114.7 2.4 %copy-start.1 = (bf16[16,12,3584]{2,0,1:T(8,128)(2,1)S(1)}, bf16[16,12,3584]{2,0,1:T(8,128)(2,1)}, u32[]{:S(2)}) copy-start(bf16[16,12,3584]{2,0,1:T(8,128)(2,1)} %fusion) | copy-start | bytes 4128772
  120.4 1.5 copy-start.3
  123.2 1.9 %copy-start.4 = (bf16[384,3712]{1,0:T(8,128)(2,1)S(1)}, bf16[384,3712]{1,0:T(8,128)(2,1)}, u32[]{:S(2)}) copy-start(bf16[384,3712]{1,0:T(8,128)(2,1)} %all-gather.6.cloned.1.call-done) | copy-start | bytes 8552452
  126.5 32.4 %collective-permute-start = (bf16[3,1792,128]{2,1,0:T(8,128)(2,1)S(1)}, bf16[3,1792,128]{2,1,0:T(8,128)(2,1)S(1)}, u32[]{:S(2)}, u32[]{:S(2)}) collective-permute-start(bf16[3,1792,128]{2,1,0:T(8,128)(2,1)S(1)} %constant_dynamic-slice_fusion), channel_id=1, source_target_pairs={{0,16},{16,0},{1,17},{17,1},{2,18},{18,2},{3,19},{19,3},{4,20},{20... | collective-permute-start | bytes 4128776 | tf_op jit(solution)/shard_map/ppermute | solution.py:92
Sparse Core Ops, SparseCore 0:
  10.8 43.5 all-gather.7
  57.1 42.8 all-gather.5
  120.6 62.9 reduce-scatter.1
